TPU v7x, 32 devices: a whole 2x2x4 slice. The times are simulated.
32 devices in a mesh: seq: 16 (over z, x, core), tp: 2 (over y).
Axes of the slice: x: 2, y: 2, z: 4, core: 2. Of those that a mesh axis runs over, the one named last changes fastest.
Arguments:
- normed_input: bfloat16 [2048, 4096], P(('seq', 'tp')), may hold values from -6 to 6
- output_gradient: bfloat16 [2048, 14336], P('seq', 'tp'), may hold values from -0.75 to 0.75
- adapter_down: bfloat16 [64, 16, 4096], P('seq', None, 'tp'), may hold values from -0.09375 to 0.09375
- adapter_up: bfloat16 [64, 16, 14336], P('seq', None, 'tp'), may hold values from -1.5 to 1.5
- adapter_of_block: int32 [16], P('seq'), may hold values from 0 to 63
- live_per_block: int32 [16], P('seq'), may hold values from 32 to 128, as said below
- adapter_home_row: int32 [64], replicated, may hold values from 0 to 63, each once
Outputs:
- adapter_output: bfloat16 [2048, 14336], P('seq', 'tp')
- input_gradient: bfloat16 [2048, 4096], P(('seq', 'tp'))
- down_gradient: float32 [64, 16, 4096], P('seq', None, 'tp')
- up_gradient: float32 [64, 16, 14336], P('seq', None, 'tp')
Inputs may be any that keep to these rules, and one draw needn't show every extreme that they name: `live_per_block`: every eighth block, counting from block 0, is full. `adapter_home_row`: each row appears once.
All inputs are finite; a program needn't handle non-finite values.
Results may differ from a plain program's by a relative error of at most 0.0051.
Values may be sent and summed in bfloat16 or wider, within the bound.
A program may use at most 128 MiB of HBM per device.

v0:
```python
import jax
import jax.numpy as jnp
from jax import lax
from jax.sharding import PartitionSpec as P

adapter_scale = 2.0


def per_device(
    normed_input,
    output_gradient,
    adapter_down,
    adapter_up,
    adapter_of_block,
    live_per_block,
    adapter_home_row,
):
    seq_count = lax.axis_size("seq")
    total_blocks = adapter_of_block.shape[0]
    token_rows = output_gradient.shape[0]
    block_length = token_rows // total_blocks
    adapters = adapter_home_row.shape[0]
    rank_projected = adapter_down.shape[1]
    width_slice = adapter_down.shape[2]
    hidden_slice = adapter_up.shape[2]
    all_a, all_b = (
        lax.all_gather(adapter_down, "seq", axis=0, tiled=True),
        lax.all_gather(adapter_up, "seq", axis=0, tiled=True),
    )
    chosen = (adapter_of_block[:, None] == jnp.arange(adapters, dtype=jnp.int32)[None, :]).astype(
        jnp.float32
    )
    chosen_low = chosen.astype(jnp.bfloat16)
    pick_a = jnp.einsum(
        "ba,ard->brd", chosen_low, all_a, preferred_element_type=jnp.float32
    ).astype(jnp.bfloat16)
    pick_b = jnp.einsum(
        "ba,arf->brf", chosen_low, all_b, preferred_element_type=jnp.float32
    ).astype(jnp.bfloat16)
    token_live_mask = (
        jnp.arange(block_length, dtype=jnp.int32)[None, :] < live_per_block[:, None]
    ).astype(jnp.float32)[:, :, None]
    g_blocks = output_gradient.reshape(total_blocks, block_length, hidden_slice)
    back_part = jnp.einsum("btf,brf->btr", g_blocks, pick_b, preferred_element_type=jnp.float32)
    back_part = back_part.reshape(total_blocks, block_length * rank_projected)
    x_tensor = lax.all_to_all(normed_input, "tp", split_axis=1, concat_axis=0, tiled=True)
    x_blocks = x_tensor.reshape(total_blocks, block_length, width_slice)
    down_part = jnp.einsum("btd,brd->btr", x_blocks, pick_a, preferred_element_type=jnp.float32)
    down_part = down_part.reshape(total_blocks, block_length * rank_projected)
    down_sum, backward_total = lax.psum((down_part, back_part), "tp")
    down_reduced = (
        down_sum.reshape(total_blocks, block_length, rank_projected) * token_live_mask
    ).astype(jnp.bfloat16)
    backward_reduced = (
        adapter_scale
        * backward_total.reshape(total_blocks, block_length, rank_projected)
        * token_live_mask
    ).astype(jnp.bfloat16)
    grad_tensor = jnp.einsum(
        "btr,brd->btd", backward_reduced, pick_a, preferred_element_type=jnp.float32
    )
    grad_tensor = grad_tensor.astype(jnp.bfloat16).reshape(token_rows, width_slice)
    input_gradient = lax.all_to_all(grad_tensor, "tp", split_axis=0, concat_axis=1, tiled=True)
    grad_a_blocks = jnp.einsum(
        "btr,btd->brd", backward_reduced, x_blocks, preferred_element_type=jnp.float32
    )
    adapter_output = adapter_scale * jnp.einsum(
        "btr,brf->btf", down_reduced, pick_b, preferred_element_type=jnp.float32
    )
    adapter_output = adapter_output.astype(jnp.bfloat16).reshape(token_rows, hidden_slice)
    up_gradient_blocks = adapter_scale * jnp.einsum(
        "btr,btf->brf", down_reduced, g_blocks, preferred_element_type=jnp.float32
    )
    block_row = jnp.dot(
        chosen, adapter_home_row.astype(jnp.float32), precision=lax.Precision.HIGHEST
    )
    slots_each = adapters // seq_count
    my_rows = (lax.axis_index("seq") * slots_each + jnp.arange(slots_each, dtype=jnp.int32)).astype(
        jnp.float32
    )
    piece_a = lax.all_gather(grad_a_blocks, "seq", axis=0, tiled=True)
    piece_b = lax.all_gather(up_gradient_blocks, "seq", axis=0, tiled=True)
    piece_rows = lax.all_gather(block_row, "seq", axis=0, tiled=True)
    match = (piece_rows[:, None] == my_rows[None, :]).astype(jnp.float32)
    following_down = jnp.einsum("ns,nrd->srd", match, piece_a, precision=lax.Precision.HIGHEST)
    following_up = jnp.einsum("ns,nrf->srf", match, piece_b, precision=lax.Precision.HIGHEST)
    return (adapter_output, input_gradient, following_down, following_up)


def solution(mesh):
    placed = (
        P(("seq", "tp"), None),
        P("seq", "tp"),
        P("seq", None, "tp"),
        P("seq", None, "tp"),
        P("seq"),
        P("seq"),
        P(),
    )
    return jax.shard_map(
        per_device,
        mesh=mesh,
        in_specs=placed,
        out_specs=(
            P("seq", "tp"),
            P(("seq", "tp"), None),
            P("seq", None, "tp"),
            P("seq", None, "tp"),
        ),
        check_vma=False,
    )
```

profile of v0, /device:TPU:1, one launch (start us, length us, event | category | flops | bytes accessed | tf_op | source)
XLA Modules:
  0.0 334.7 jit_solution(5447570768813441117)
XLA Ops:
  7.2 0.0 copy-start
  7.2 0.0 all-gather.7.cloned.1.call-start
  7.2 0.7 all-gather.7.cloned.1.call-update
  7.9 0.0 all-gather.9.cloned.1.call-start
  8.0 0.7 all-gather.9.cloned.1.call-update
  8.7 1.9 copy.62
  10.5 3.5 %all-to-all-start = ((bf16[64,2,2048]{2,0,1:T(8,128)(2,1)}), bf16[64,2,2048]{2,0,1:T(8,128)(2,1)S(1)}, u32[]{:S(2)}, u32[]{:S(2)}) async-start(bf16[64,2,2048]{2,0,1:T(8,128)(2,1)} %bitcast.50), calls=%async_computation | async-start | bytes 1048576 | tf_op jit(solution)/shard_map/all_to_all | solution.py:46
  14.0 0.0 all-gather.11.cloned.1.call-start
  15.4 0.1 mul.64
  15.5 0.1 mul.65
  15.6 0.1 mul.57
  15.7 0.1 mul.58
  15.8 47.3 %all-gather.7.cloned.1.call-done = bf16[64,16,2048]{2,1,0:T(8,128)(2,1)} async-done(((bf16[4,16,2048]{2,1,0:T(8,128)(2,1)}), bf16[64,16,2048]{2,1,0:T(8,128)(2,1)}) %all-gather.7.cloned.1.call-update) | async-done | bytes 4194320 | tf_op jit(solution)/shard_map/all_gather | solution.py:27
  63.0 6.7 %fusion.5 = bf16[1,16,2048]{2,0,1:T(2,128)(2,1)S(1)} fusion(bf16[64,16,2048]{2,1,0:T(8,128)(2,1)} %all-gather.7.cloned.1.call-done, s32[]{:T(128)} %bitcast.51), kind=kOutput, calls=%fused_computation.7 | convolution fusion | flops 4194496 | bytes 4259844 | tf_op jit(solution)/shard_map/ba,ard->brd/dot_general | solution.py:34
  69.7 0.0 all-to-all-done
  69.7 0.3 convolution_bitcast_fusion.1
  70.0 0.1 copy.32
  70.1 0.1 reshape.142
  70.2 107.1 %all-gather.9.cloned.1.call-done = bf16[64,16,7168]{2,1,0:T(8,128)(2,1)} async-done(((bf16[4,16,7168]{2,1,0:T(8,128)(2,1)}), bf16[64,16,7168]{2,1,0:T(8,128)(2,1)}) %all-gather.9.cloned.1.call-update) | async-done | bytes 14680080 | tf_op jit(solution)/shard_map/all_gather | solution.py:28
  177.2 20.9 %fusion = bf16[1,16,7168]{2,0,1:T(2,128)(2,1)S(1)} fusion(bf16[64,16,7168]{2,1,0:T(8,128)(2,1)} %all-gather.9.cloned.1.call-done, s32[]{:T(128)} %bitcast.52), kind=kOutput, calls=%fused_computation | convolution fusion | flops 14680256 | bytes 14909444 | tf_op jit(solution)/shard_map/ba,arf->brf/dot_general | solution.py:37
  198.1 0.0 copy-done
  198.1 0.0 copy-start.2
  198.2 0.0 copy-start.1
  198.2 0.6 convolution_bitcast_fusion
  198.7 0.1 copy.33
  198.9 0.1 reshape.143
  199.0 6.0 %all-reduce.1 = (f32[1,2048]{1,0:T(1,128)S(1)}, f32[1,2048]{1,0:T(1,128)S(1)}) all-reduce(f32[1,2048]{1,0:T(1,128)S(1)} %reshape.142, f32[1,2048]{1,0:T(1,128)S(1)} %reshape.143), channel_id=1, replica_groups=mesh['seq'=16,'tp'=2] {'tp'}, use_global_device_ids=true, to_apply=%region_0.0 | all-reduce | flops 4096 | bytes 32768 | tf_op jit(solution)/shard_map/psum | solution.py:50
  205.0 0.1 convert_reduce_fusion
  205.0 0.1 convert_element_type.81
  205.1 0.9 fusion.24
  206.0 0.0 all-gather.11.cloned.1.call-update
  206.0 0.0 all-gather.13.cloned.1.call-start
  206.1 0.1 convert_element_type.77
  206.2 1.2 convolution_multiply_fusion.1
  207.3 0.0 all-gather.13.cloned.1.call-update
  207.4 0.0 copy-done.2
  207.4 0.6 dynamic-slice
  208.0 0.0 copy-done.1
  208.0 0.6 fusion.19
  208.6 1.4 dynamic-update-slice
  210.0 31.4 %all-reduce = f32[16]{0:T(128)S(1)} all-reduce(f32[16]{0:T(128)S(1)} %dynamic-update-slice), channel_id=1, replica_groups=mesh['seq'=16,'tp'=2] {'seq'}, use_global_device_ids=true, to_apply=%add | all-reduce | flops 16 | bytes 128
  241.4 1.1 convolution_convert_fusion
  242.5 3.7 %all-to-all-start.1 = ((bf16[2,64,2048]{2,1,0:T(8,128)(2,1)}), bf16[2,64,2048]{2,1,0:T(8,128)(2,1)S(1)}, u32[]{:S(2)}, u32[]{:S(2)}) async-start(bf16[2,64,2048]{2,1,0:T(8,128)(2,1)} %bitcast.10), calls=%async_computation.1 | async-start | bytes 1048576 | tf_op jit(solution)/shard_map/all_to_all | solution.py:63
  246.2 1.9 fusion.2
  248.0 5.1 %all-to-all-done.1 = bf16[2,64,2048]{2,1,0:T(8,128)(2,1)S(1)} async-done(((bf16[2,64,2048]{2,1,0:T(8,128)(2,1)}), bf16[2,64,2048]{2,1,0:T(8,128)(2,1)S(1)}, u32[]{:S(2)}, u32[]{:S(2)}) %all-to-all-start.1) | async-done | bytes 524320 | tf_op jit(solution)/shard_map/all_to_all | solution.py:63
  253.2 0.8 copy.46
  254.0 0.0 all-gather.11.cloned.1.call-done
  254.0 3.5 %fusion.7 = f32[4,16,2048]{2,0,1:T(4,128)S(1)} fusion(f32[16,16,2048]{2,1,0:T(8,128)} %bitcast.59, f32[16]{0:T(128)S(1)} %all-reduce, f32[4]{0:T(128)S(1)} %add_convert_fusion), kind=kOutput, calls=%fused_computation.10 | convolution fusion | flops 25165888 | bytes 2621520 | tf_op jit(solution)/shard_map/ns,nrd->srd/dot_general | solution.py:85
  257.5 1.1 copy.37
  258.6 57.7 %all-gather.13.cloned.1.call-done = f32[256,7168]{1,0:T(8,128)} async-done(((f32[16,7168]{1,0:T(8,128)}), f32[256,7168]{1,0:T(8,128)}) %all-gather.13.cloned.1.call-update) | async-done | bytes 7340048 | tf_op jit(solution)/shard_map/all_gather | solution.py:82
  316.3 9.5 %fusion.3 = f32[4,16,7168]{2,0,1:T(4,128)S(1)} fusion(f32[16,16,7168]{2,1,0:T(8,128)} %bitcast.56, f32[16]{0:T(128)S(1)} %all-reduce, f32[4]{0:T(128)S(1)} %add_convert_fusion), kind=kOutput, calls=%fused_computation.5 | convolution fusion | flops 88080448 | bytes 9175120 | tf_op jit(solution)/shard_map/ns,nrf->srf/dot_general | solution.py:86
  325.8 2.3 copy.38
  (4 shorter events, 0.0 us)
Async XLA Ops:
  7.2 191.0 %copy-start = (bf16[128,7168]{1,0:T(8,128)(2,1)S(1)}, bf16[128,7168]{1,0:T(8,128)(2,1)}, u32[]{:S(2)}) copy-start(bf16[128,7168]{1,0:T(8,128)(2,1)} %param.8) | copy-start | bytes 5505028
  7.2 55.8 %all-gather.7.cloned.1.call-start = ((), (), s32[]{:S(2)}) async-start(), calls=%async_computation.2 | async-start | bytes 4456448 | tf_op jit(solution)/shard_map/all_gather | solution.py:27
  7.9 169.3 %all-gather.9.cloned.1.call-start = ((), (), s32[]{:S(2)}) async-start(), calls=%async_computation.3 | async-start | bytes 15597568 | tf_op jit(solution)/shard_map/all_gather | solution.py:28
  10.5 59.2 %all-to-all-start = ((bf16[64,2,2048]{2,0,1:T(8,128)(2,1)}), bf16[64,2,2048]{2,0,1:T(8,128)(2,1)S(1)}, u32[]{:S(2)}, u32[]{:S(2)}) async-start(bf16[64,2,2048]{2,0,1:T(8,128)(2,1)} %bitcast.50), calls=%async_computation | async-start | bytes 1048576 | tf_op jit(solution)/shard_map/all_to_all | solution.py:46
  14.0 240.0 %all-gather.11.cloned.1.call-start = ((), (), s32[]{:S(2)}) async-start(), calls=%async_computation.4 | async-start | bytes 2228224 | tf_op jit(solution)/shard_map/all_gather | solution.py:81
  198.1 9.2 %copy-start.2 = (u32[32]{0:T(128)S(1)}, u32[32]{0:T(128)}, u32[]{:S(2)}) copy-start(u32[32]{0:T(128)} %constant.20) | copy-start | bytes 388
  198.2 9.8 %copy-start.1 = (s32[64]{0:T(128)S(1)}, s32[64]{0:T(128)}, u32[]{:S(2)}) copy-start(s32[64]{0:T(128)} %param.13) | copy-start | bytes 772
  206.0 110.3 %all-gather.13.cloned.1.call-start = ((), (), s32[]{:S(2)}) async-start(), calls=%async_computation.5 | async-start | bytes 7798784 | tf_op jit(solution)/shard_map/all_gather | solution.py:82
  242.5 10.7 %all-to-all-start.1 = ((bf16[2,64,2048]{2,1,0:T(8,128)(2,1)}), bf16[2,64,2048]{2,1,0:T(8,128)(2,1)S(1)}, u32[]{:S(2)}, u32[]{:S(2)}) async-start(bf16[2,64,2048]{2,1,0:T(8,128)(2,1)} %bitcast.10), calls=%async_computation.1 | async-start | bytes 1048576 | tf_op jit(solution)/shard_map/all_to_all | solution.py:63
Sparse Core Ops, SparseCore 0:
  10.1 52.8 all-gather.6
  65.3 111.8 all-gather.8
  206.2 40.7 all-gather.10
  249.7 66.5 all-gather.12
where the time goes:
time: 335 us
  waiting for transfers between devices  219 us (65%)
  matrix products  46.4 us (14%)
  blocking collectives  37.4 us (11%)
  between operations  15.2 us (5%)
  local copies, waits for them, and re-layouts  9.02 us (3%)
  starting transfers between devices  7.36 us (2%)
    all_gather x1, waiting for transfers between devices, per_device(): lax.all_gather(adapter_up, 'seq', axis=0, tiled=True)  107 us
    all_gather x1, waiting for transfers between devices, per_device(): piece_b = lax.all_gather(up_gradient_blocks, 'seq', axis=0, tiled=True)  57.7 us
    all_gather x1, waiting for transfers between devices, per_device(): lax.all_gather(adapter_down, 'seq', axis=0, tiled=True)  47.3 us
    unnamed x1, blocking collectives  31.4 us
    dot_general x1, matrix products, per_device(): jnp.einsum('ba,arf->brf', chosen_low, all_b, preferred_element_type=jnp.f...  20.9 us
    dot_general x1, matrix products, per_device(): jnp.einsum('ns,nrf->srf', match, piece_b, precision=lax.Precision.HIGHEST)  9.53 us
    dot_general x1, matrix products, per_device(): jnp.einsum('ba,ard->brd', chosen_low, all_a, preferred_element_type=jnp.f...  6.7 us
  transfers between devices with their start and end apart: 6, of which 4 were waited for; matrix products, arithmetic and copies ran while one was open for 6% of the time, Pallas kernels for 0%

commit v1 on v0

v1 whole, which is shorter than its diff:
```python
import functools

import jax
import jax.numpy as jnp
from jax import lax
from jax.experimental import pallas as pl
from jax.experimental.pallas import tpu as pltpu
from jax.sharding import PartitionSpec as P

adapter_scale = 2.0
GROUP = 4
MESH = pl.DeviceIdType.MESH
VMEM = pltpu.VMEM


def pieces(width, most):
    tiles = width // 128
    count = max(k for k in range(1, most + 1) if tiles % k == 0)
    step = width // count
    return [(i * step, step) for i in range(count)]


def greet(n, tp, me, mine):
    barrier = pltpu.get_barrier_semaphore()

    def seq_signal(d, carry):
        pl.semaphore_signal(barrier, inc=1, device_id=(lax.rem(me + d, n), mine), device_id_type=MESH)
        return carry

    lax.fori_loop(1, n, seq_signal, 0)
    for d in range(1, tp):
        pl.semaphore_signal(barrier, inc=1, device_id=(me, lax.rem(mine + d, tp)), device_id_type=MESH)
    pl.semaphore_wait(barrier, n - 1 + tp - 1)


def factor_kernel(
    n, tp, a_ref, b_ref, x_ref, id_ref,
    a_out, b_out, x_out, id_out,
    fa, fb, sa, sb, za, zb,
    raw_send, raw_recv, z_send, z_recv, id_send, id_recv, x_send, x_recv,
):
    me, mine = lax.axis_index("seq"), lax.axis_index("tp")
    planes = n // GROUP
    plane, spot = me // GROUP, lax.rem(me, GROUP)
    near = me + 1 - 2 * lax.rem(spot, 2)
    far = me + 2 - 4 * (spot // 2)
    far_spot = spot + 2 - 4 * (spot // 2)
    rows = a_ref.shape[0]
    rank = a_out.shape[0]
    total = fa.shape[0]
    width = x_out.shape[2]
    greet(n, tp, me, mine)

    def remote(src, dst, send, recv, seq_at, tp_at):
        return pltpu.make_async_remote_copy(
            src_ref=src, dst_ref=dst, send_sem=send, recv_sem=recv,
            device_id=(seq_at, tp_at), device_id_type=MESH,
        )

    def id_copy(d):
        return remote(id_ref, id_out.at[me], id_send.at[d], id_recv.at[d], lax.rem(me + d, n), mine)

    lax.fori_loop(1, n, lambda d, c: (id_copy(d).start(), c)[1], 0)

    cuts = [(a_ref, fa, sa, za, a_out, *cut) for cut in pieces(a_ref.shape[1], 2)]
    cuts += [(b_ref, fb, sb, zb, b_out, *cut) for cut in pieces(b_ref.shape[1], 7)]
    own = pl.ds(pl.multiple_of(spot * rows, rows), rows)
    other = pl.ds(pl.multiple_of(far_spot * rows, rows), rows)
    to_far, to_near, forward = [], [], []
    for j, (src, full, _, _, _, start, size) in enumerate(cuts):
        cols = pl.ds(start, size)
        to_far.append(remote(src.at[:, cols], full.at[own, cols], raw_send.at[0, j], raw_recv.at[0, j], far, mine))
        to_near.append(remote(src.at[:, cols], full.at[own, cols], raw_send.at[1, j], raw_recv.at[1, j], near, mine))
        forward.append(remote(full.at[other, cols], full.at[other, cols], raw_send.at[2, j], raw_recv.at[2, j], near, mine))
        to_far[j].start()
        to_near[j].start()
    x_copies = []
    for d in range(1, tp):
        peer = lax.rem(mine + d, tp)
        copy = remote(
            x_ref.at[:, pl.ds(pl.multiple_of(peer * width, width), width)], x_out.at[mine],
            x_send.at[d], x_recv.at[d], me, peer,
        )
        copy.start()
        x_copies.append(copy)
    x_out[mine] = x_ref[:, pl.ds(pl.multiple_of(mine * width, width), width)]
    id_out[me] = id_ref[...]
    fa[own, :] = a_ref[...]
    fb[own, :] = b_ref[...]
    lax.fori_loop(1, n, lambda d, c: (id_copy(d).wait(), c)[1], 0)

    base = plane * (total // rank)
    row_at = lax.broadcasted_iota(jnp.int32, (rank, total), 0)
    col_at = lax.broadcasted_iota(jnp.int32, (rank, total), 1)
    picks = []
    for p in range(planes):
        wanted = jnp.broadcast_to(id_out[p * GROUP + spot, 0:1, 0:1], (rank, total)) - base
        picks.append((col_at == wanted * rank + row_at).astype(jnp.float32))
    pick = jnp.concatenate(picks, axis=0).astype(jnp.bfloat16)

    z_copies = []
    for j, (_, full, chosen, landed, _, start, size) in enumerate(cuts):
        cols = pl.ds(start, size)
        to_far[j].wait_recv()
        forward[j].start()
        to_near[j].wait_recv()
        forward[j].wait_recv()
        got = jnp.dot(pick, full[:, cols], preferred_element_type=jnp.float32).astype(jnp.bfloat16)
        chosen[:, :, cols] = got.reshape(planes, rank, size)
        for d in range(1, planes):
            to = lax.rem(plane + d, planes)
            copy = remote(
                chosen.at[to, :, cols], landed.at[d, :, cols],
                z_send.at[d, j], z_recv.at[d, j], to * GROUP + spot, mine,
            )
            copy.start()
            z_copies.append(copy)
    for j, (_, _, chosen, landed, out, start, size) in enumerate(cuts):
        cols = pl.ds(start, size)
        value = chosen[plane, :, cols].astype(jnp.float32)
        for d in range(1, planes):
            z_copies[j * (planes - 1) + d - 1].wait_recv()
            value += landed[d, :, cols].astype(jnp.float32)
        out[:, cols] = value.astype(jnp.bfloat16)
    for copy in x_copies:
        copy.wait()
    for copy in to_far + to_near + forward + z_copies:
        copy.wait_send()


def fetch_factors(n, tp, a, b, x, ids):
    slots, rank, width = a.shape
    hidden = b.shape[2]
    tokens = x.shape[0]
    planes = n // GROUP
    cuts = len(pieces(width, 2)) + len(pieces(hidden, 7))
    total = GROUP * slots * rank
    low = jnp.bfloat16
    dma = pltpu.SemaphoreType.DMA
    return pl.pallas_call(
        functools.partial(factor_kernel, n, tp),
        out_shape=(
            jax.ShapeDtypeStruct((rank, width), low),
            jax.ShapeDtypeStruct((rank, hidden), low),
            jax.ShapeDtypeStruct((tp, tokens, width), low),
            jax.ShapeDtypeStruct((n, 8, 128), jnp.int32),
        ),
        in_specs=[pl.BlockSpec(memory_space=VMEM)] * 4,
        out_specs=(pl.BlockSpec(memory_space=VMEM),) * 4,
        scratch_shapes=[
            VMEM((total, width), low), VMEM((total, hidden), low),
            VMEM((planes, rank, width), low), VMEM((planes, rank, hidden), low),
            VMEM((planes, rank, width), low), VMEM((planes, rank, hidden), low),
            dma((3, cuts)), dma((3, cuts)), dma((planes, cuts)), dma((planes, cuts)),
            dma((n,)), dma((n,)), dma((tp,)), dma((tp,)),
        ],
        compiler_params=pltpu.CompilerParams(
            collective_id=0, has_side_effects=True, vmem_limit_bytes=48 * 1024 * 1024
        ),
    )(a.reshape(slots * rank, width), b.reshape(slots * rank, hidden), x, ids)


def gradient_kernel(
    n, tp, ga_ref, gb_ref, gx_ref, place_ref,
    a_out, b_out, x_out,
    fa, fb,
    z_send, z_recv, far_send, far_recv, x_send, x_recv,
):
    me, mine = lax.axis_index("seq"), lax.axis_index("tp")
    planes = n // GROUP
    plane, spot = me // GROUP, lax.rem(me, GROUP)
    near = me + 1 - 2 * lax.rem(spot, 2)
    far = me + 2 - 4 * (spot // 2)
    far_spot = spot + 2 - 4 * (spot // 2)
    rank = ga_ref.shape[0]
    width = gx_ref.shape[2]
    column = planes * rank
    greet(n, tp, me, mine)

    def remote(src, dst, send, recv, seq_at, tp_at):
        return pltpu.make_async_remote_copy(
            src_ref=src, dst_ref=dst, send_sem=send, recv_sem=recv,
            device_id=(seq_at, tp_at), device_id_type=MESH,
        )

    cuts = [(gb_ref, fb, b_out, *cut) for cut in pieces(gb_ref.shape[1], 7)]
    cuts += [(ga_ref, fa, a_out, *cut) for cut in pieces(ga_ref.shape[1], 2)]
    row = spot * column + plane * rank
    slot = pl.ds(pl.multiple_of(row, rank), rank)
    own = pl.ds(pl.multiple_of(spot * column, column), column)
    other = pl.ds(pl.multiple_of(far_spot * column, column), column)
    z_copies, to_far, to_near, forward = [], [], [], []
    for j, (src, full, _, start, size) in enumerate(cuts):
        cols = pl.ds(start, size)
        for d in range(1, planes):
            copy = remote(
                src.at[:, cols], full.at[slot, cols], z_send.at[d, j], z_recv.at[d, j],
                lax.rem(plane + d, planes) * GROUP + spot, mine,
            )
            copy.start()
            z_copies.append(copy)
    x_copies = []
    for d in range(1, tp):
        peer = lax.rem(mine + d, tp)
        copy = remote(
            gx_ref.at[peer], x_out.at[:, pl.ds(pl.multiple_of(mine * width, width), width)],
            x_send.at[d], x_recv.at[d], me, peer,
        )
        copy.start()
        x_copies.append(copy)
    x_out[:, pl.ds(pl.multiple_of(mine * width, width), width)] = gx_ref[mine]
    fa[slot, :] = ga_ref[...]
    fb[slot, :] = gb_ref[...]

    def finish(j):
        _, full, out, start, size = cuts[j]
        cols = pl.ds(start, size)
        to_near[j].wait_recv()
        forward[j].wait_recv()
        out[:, cols] = jnp.dot(place_ref[...], full[:, cols], preferred_element_type=jnp.float32)

    def pass_on(j):
        to_far[j].wait_recv()
        forward[j].start()

    for j, (src, full, out, start, size) in enumerate(cuts):
        cols = pl.ds(start, size)
        for d in range(1, planes):
            z_copies[j * (planes - 1) + d - 1].wait_recv()
        to_far.append(remote(full.at[own, cols], full.at[own, cols], far_send.at[0, j], far_recv.at[0, j], far, mine))
        to_near.append(remote(full.at[own, cols], full.at[own, cols], far_send.at[1, j], far_recv.at[1, j], near, mine))
        forward.append(remote(full.at[other, cols], full.at[other, cols], far_send.at[2, j], far_recv.at[2, j], near, mine))
        to_far[j].start()
        to_near[j].start()
        if j >= 1:
            pass_on(j - 1)
        if j >= 2:
            finish(j - 2)
    last = len(cuts) - 1
    pass_on(last)
    finish(last - 1)
    finish(last)
    for copy in x_copies:
        copy.wait()
    for copy in to_far + to_near + forward + z_copies:
        copy.wait_send()


def deliver_gradients(n, tp, ga, gb, gx, place):
    rank, width = ga.shape
    hidden = gb.shape[1]
    tokens = gx.shape[1]
    planes = n // GROUP
    cuts = len(pieces(width, 2)) + len(pieces(hidden, 7))
    total = n * rank
    mine = place.shape[0]
    low = jnp.bfloat16
    dma = pltpu.SemaphoreType.DMA
    return pl.pallas_call(
        functools.partial(gradient_kernel, n, tp),
        out_shape=(
            jax.ShapeDtypeStruct((mine, width), jnp.float32),
            jax.ShapeDtypeStruct((mine, hidden), jnp.float32),
            jax.ShapeDtypeStruct((tokens, tp * width), low),
        ),
        in_specs=[pl.BlockSpec(memory_space=VMEM)] * 4,
        out_specs=(pl.BlockSpec(memory_space=VMEM),) * 3,
        scratch_shapes=[
            VMEM((total, width), low), VMEM((total, hidden), low),
            dma((planes, cuts)), dma((planes, cuts)), dma((3, cuts)), dma((3, cuts)),
            dma((tp,)), dma((tp,)),
        ],
        compiler_params=pltpu.CompilerParams(
            collective_id=1, has_side_effects=True, vmem_limit_bytes=48 * 1024 * 1024
        ),
    )(ga, gb, gx, place)


def per_device(
    normed_input,
    output_gradient,
    adapter_down,
    adapter_up,
    adapter_of_block,
    live_per_block,
    adapter_home_row,
):
    n, tp = lax.axis_size("seq"), lax.axis_size("tp")
    slots, rank, width = adapter_down.shape
    hidden = adapter_up.shape[2]
    token_rows = output_gradient.shape[0]
    adapters = adapter_home_row.shape[0]
    planes = n // GROUP
    f32, low = jnp.float32, jnp.bfloat16
    ids = jnp.broadcast_to(adapter_of_block[0], (8, 128))
    pick_a, pick_b, x, all_ids = fetch_factors(n, tp, adapter_down, adapter_up, normed_input, ids)
    x = x.reshape(token_rows, width)
    g = output_gradient

    block_ids = all_ids[:, 0, 0]
    chosen = block_ids[:, None] == jnp.arange(adapters, dtype=jnp.int32)[None, :]
    block_row = jnp.sum(jnp.where(chosen, adapter_home_row[None, :], 0), axis=1)
    block_row = block_row.reshape(planes, GROUP).T.reshape(n)
    out_at = jnp.arange(slots * rank, dtype=jnp.int32)
    in_at = jnp.arange(n * rank, dtype=jnp.int32)
    my_row = lax.axis_index("seq") * slots + out_at // rank
    place = (
        (jnp.repeat(block_row, rank)[None, :] == my_row[:, None])
        & ((in_at % rank)[None, :] == (out_at % rank)[:, None])
    ).astype(low)

    part = jnp.concatenate(
        [
            jnp.einsum("rd,td->rt", pick_a, x, preferred_element_type=f32),
            jnp.einsum("rf,tf->rt", pick_b, g, preferred_element_type=f32),
        ],
        axis=0,
    )
    both = part
    for d in range(1, tp):
        both = both + lax.ppermute(part, "tp", [(i, (i + d) % tp) for i in range(tp)])
    live = (jnp.arange(token_rows, dtype=jnp.int32) < live_per_block[0]).astype(f32)[None, :]
    down = (both[:rank] * live).astype(low)
    back = (adapter_scale * both[rank:] * live).astype(low)
    gb = (adapter_scale * jnp.dot(down, g, preferred_element_type=f32)).astype(low)
    ga = jnp.dot(back, x, preferred_element_type=f32).astype(low)
    gx = jnp.einsum("rt,rd->td", back, pick_a, preferred_element_type=f32).astype(low)
    out = (adapter_scale * jnp.einsum("rt,rf->tf", down, pick_b, preferred_element_type=f32)).astype(low)
    grad_a, grad_b, gx = deliver_gradients(n, tp, ga, gb, gx.reshape(tp, token_rows // tp, width), place)
    return (out, gx, grad_a.reshape(slots, rank, width), grad_b.reshape(slots, rank, hidden))


def solution(mesh):
    placed = (
        P(("seq", "tp"), None),
        P("seq", "tp"),
        P("seq", None, "tp"),
        P("seq", None, "tp"),
        P("seq"),
        P("seq"),
        P(),
    )
    return jax.shard_map(
        per_device,
        mesh=mesh,
        in_specs=placed,
        out_specs=(
            P("seq", "tp"),
            P(("seq", "tp"), None),
            P("seq", None, "tp"),
            P("seq", None, "tp"),
        ),
        check_vma=False,
    )
```

time: 335 us -> 97.6 us (0.29)
  waiting for transfers between devices: 219 us -> 0.01 us
  Pallas kernels: 0 us -> 83.4 us
  matrix products: 46.4 us -> 3.58 us
  blocking collectives: 37.4 us -> 0 us
  between operations: 15.2 us -> 2.17 us
  starting transfers between devices: 7.36 us -> 1.14 us
    all_gather x4 -> x0, waiting for transfers between devices: 212 us -> none  [the longest x1 107 us: per_device(): lax.all_gather(adapter_up, 'seq', axis=0, tiled=True)]
    pallas_call x0 -> x2, Pallas kernels: none -> 83.4 us  [the longest x1 43.8 us: deliver_gradients(): pl.pallas_call(functools.partial(gradient_kernel, n, tp), out_shape=(jax....]
    dot_general x10 -> x6, matrix products: 46.4 us -> 3.58 us  [the longest x1 1.89 us: per_device(): jnp.einsum('rt,rf->tf', down, pick_b, preferred_element_type=f32)]
    unnamed x1 -> x0, blocking collectives: 31.4 us -> none
    all_to_all x2 -> x0, starting transfers between devices: 7.2 us -> none  [the longest x1 3.71 us: per_device(): lax.all_to_all(grad_tensor, 'tp', split_axis=0, concat_axis=1, tiled=True)]
    psum x1 -> x0, blocking collectives: 6.04 us -> none  [per_device(): down_sum, backward_total = lax.psum((down_part, back_part), 'tp')]
    all_to_all x2 -> x0, waiting for transfers between devices: 5.15 us -> none  [the longest x1 5.15 us: per_device(): lax.all_to_all(grad_tensor, 'tp', split_axis=0, concat_axis=1, tiled=True)]
  transfers between devices with their start and end apart: 6 -> 1, of which waited for: 4 -> 0; matrix products, arithmetic and copies ran while one was open for 6% -> 1% of each run, Pallas kernels for 0% -> 0%
where the time goes in v1:
time: 97.6 us; the launch traced here: 97.4 us
  Pallas kernels  83.4 us (85%)
  local copies, waits for them, and re-layouts  6.8 us (7%)
  matrix products  3.58 us (4%)
  between operations  2.17 us (2%)
  starting transfers between devices  1.14 us (1%)
    pallas_call x1, Pallas kernels, deliver_gradients(): pl.pallas_call(functools.partial(gradient_kernel, n, tp), out_shape=(jax....  43.8 us
    pallas_call x1, Pallas kernels, fetch_factors(): pl.pallas_call(functools.partial(factor_kernel, n, tp), out_shape=(jax.Sh...  39.6 us
    unnamed x13, local copies, waits for them, and re-layouts  5.99 us
  transfers between devices with their start and end apart: 1, of which 0 were waited for; matrix products, arithmetic and copies ran while one was open for 1% of the time, Pallas kernels for 0%

profile of v1, /device:TPU:1, one launch (start us, length us, event | category | flops | bytes accessed | tf_op | source)
XLA Modules:
  0.0 97.4 jit_solution(5847121739586853304)
XLA Ops:
  0.6 0.0 copy-start
  1.4 0.0 copy-start.1
  1.4 1.2 %copy-done.1 = bf16[4,16,7168]{2,1,0:T(8,128)(2,1)S(1)} copy-done((bf16[4,16,7168]{2,1,0:T(8,128)(2,1)S(1)}, bf16[4,16,7168]{2,1,0:T(8,128)(2,1)}, u32[]{:S(2)}) %copy-start.1) | copy-done | bytes 917528
  2.6 0.0 copy-start.2
  2.6 1.0 %copy-done.2 = bf16[64,4096]{1,0:T(8,128)(2,1)S(1)} copy-done((bf16[64,4096]{1,0:T(8,128)(2,1)S(1)}, bf16[64,4096]{1,0:T(8,128)(2,1)}, u32[]{:S(2)}) %copy-start.2) | copy-done | bytes 524312
  3.7 0.0 copy-start.3
  3.7 0.9 copy-done.3
  4.6 0.0 copy-start.4
  4.6 39.6 %shard_map.102 = (bf16[16,2048]{1,0:T(8,128)(2,1)S(1)}, bf16[16,7168]{1,0:T(8,128)(2,1)S(1)}, bf16[2,64,2048]{2,1,0:T(8,128)(2,1)S(1)}, s32[16,8,128]{2,1,0:T(8,128)S(1)}) custom-call(bf16[64,2048]{1,0:T(8,128)(2,1)S(1)} %bitcast.26, bf16[64,7168]{1,0:T(8,128)(2,1)S(1)} %bitcast.24, bf16[64,4096]{1,0:T(8,128)(2,1)S(1)} %copy-done.2, ...), custom_call_target="tpu_custom_call" | custom-call | tf_op jit(solution)/shard_map/pallas_call | solution.py:140
  44.2 0.2 fusion.10
  44.5 0.0 copy-done
  44.5 0.6 fusion.11
  45.1 1.1 %collective-permute-start = (f32[32,128]{1,0:T(8,128)S(1)}, f32[32,128]{1,0:T(8,128)S(1)}, u32[]{:S(2)}, u32[]{:S(2)}) collective-permute-start(f32[32,128]{1,0:T(8,128)S(1)} %pad_maximum_fusion), channel_id=1, source_target_pairs={{0,1},{1,0},{2,3},{3,2},{4,5},{5,4},{6,7},{7,6},{8,9},{9,8},{10,11... | collective-permute-start | bytes 49160 | tf_op jit(solution)/shard_map/ppermute | solution.py:321
  46.9 0.4 slice_reduce_fusion
  47.3 0.0 copy-done.4
  47.3 0.2 select_reduce_fusion
  47.5 0.1 reshape.76
  47.5 0.1 copy.13
  47.6 0.1 reshape.77
  47.7 0.1 broadcast_in_dim.27
  47.8 0.1 eq.51
  47.9 0.1 and_convert_fusion.place_ref
  48.0 0.0 collective-permute-done
  48.0 0.3 convolution_convert_fusion
  48.4 0.2 convolution_convert_fusion.1.ga_ref
  48.5 0.4 fusion.1.gb_ref
  48.9 1.9 %fusion = bf16[128,7168]{1,0:T(8,128)(2,1)} fusion(bf16[16,7168]{1,0:T(8,128)(2,1)S(1)} %get-tuple-element.13, f32[32,128]{1,0:T(8,128)S(1)} %fusion.9, f32[128]{0:T(128)S(1)} %compare_convert_fusion), kind=kOutput, calls=%fused_computation.1 | convolution fusion | flops 31199232 | bytes 2073088 | tf_op jit(solution)/shard_map/rt,rf->tf/dot_general | solution.py:328
  50.8 43.8 %shard_map.103 = (f32[64,2048]{1,0:T(8,128)S(1)}, f32[64,7168]{1,0:T(8,128)S(1)}, bf16[64,4096]{1,0:T(8,128)(2,1)S(1)}) custom-call(bf16[16,2048]{1,0:T(8,128)(2,1)S(1)} %convolution_convert_fusion.1.ga_ref, bf16[16,7168]{1,0:T(8,128)(2,1)S(1)} %fusion.1.gb_ref, bf16[2,64,2048]{2,1,0:T(8,128)(2,1)S(1)} %bitcast.22, bf16[64,256]{1,0:T(8,128)(2,1)S(1)} %and_convert_fusion.place_ref), custom_call_target="tpu_custom_call" | custom-call | tf_op jit(solution)/shard_map/pallas_call | solution.py:259
  94.6 0.8 copy.19
  95.4 0.8 copy.20
  96.2 1.2 %copy.21 = f32[4,16,7168]{2,1,0:T(8,128)} copy(f32[4,16,7168]{2,1,0:T(8,128)S(1)} %bitcast.23) | data formatting | bytes 3670016
  (7 shorter events, 0.0 us)
Async XLA Ops:
  0.6 43.9 %copy-start = (bf16[128,7168]{1,0:T(8,128)(2,1)S(1)}, bf16[128,7168]{1,0:T(8,128)(2,1)}, u32[]{:S(2)}) copy-start(bf16[128,7168]{1,0:T(8,128)(2,1)} %param.8) | copy-start | bytes 5505028
  1.4 1.2 %copy-start.1 = (bf16[4,16,7168]{2,1,0:T(8,128)(2,1)S(1)}, bf16[4,16,7168]{2,1,0:T(8,128)(2,1)}, u32[]{:S(2)}) copy-start(bf16[4,16,7168]{2,1,0:T(8,128)(2,1)} %param.10) | copy-start | bytes 2752516
  2.6 1.0 %copy-start.2 = (bf16[64,4096]{1,0:T(8,128)(2,1)S(1)}, bf16[64,4096]{1,0:T(8,128)(2,1)}, u32[]{:S(2)}) copy-start(bf16[64,4096]{1,0:T(8,128)(2,1)} %x_ref.1) | copy-start | bytes 1572868
  3.7 0.9 copy-start.3
  4.6 42.7 %copy-start.4 = (s32[64]{0:T(128)S(1)}, s32[64]{0:T(128)}, u32[]{:S(2)}) copy-start(s32[64]{0:T(128)} %param.13) | copy-start | bytes 772
  45.1 2.9 %collective-permute-start = (f32[32,128]{1,0:T(8,128)S(1)}, f32[32,128]{1,0:T(8,128)S(1)}, u32[]{:S(2)}, u32[]{:S(2)}) collective-permute-start(f32[32,128]{1,0:T(8,128)S(1)} %pad_maximum_fusion), channel_id=1, source_target_pairs={{0,1},{1,0},{2,3},{3,2},{4,5},{5,4},{6,7},{7,6},{8,9},{9,8},{10,11... | collective-permute-start | bytes 49160 | tf_op jit(solution)/shard_map/ppermute | solution.py:321

commit v2 on v0

v2 whole, which is shorter than its diff:
```python
import functools

import jax
import jax.numpy as jnp
from jax import lax
from jax.experimental import pallas as pl
from jax.experimental.pallas import tpu as pltpu
from jax.sharding import PartitionSpec as P

adapter_scale = 2.0
GROUP = 4
MESH = pl.DeviceIdType.MESH
VMEM = pltpu.VMEM


def pieces(width, most):
    tiles = width // 128
    count = max(k for k in range(1, most + 1) if tiles % k == 0)
    step = width // count
    return [(i * step, step) for i in range(count)]


def greet(n, tp, me, mine):
    barrier = pltpu.get_barrier_semaphore()

    def seq_signal(d, carry):
        pl.semaphore_signal(barrier, inc=1, device_id=(lax.rem(me + d, n), mine), device_id_type=MESH)
        return carry

    lax.fori_loop(1, n, seq_signal, 0)
    for d in range(1, tp):
        pl.semaphore_signal(barrier, inc=1, device_id=(me, lax.rem(mine + d, tp)), device_id_type=MESH)
    pl.semaphore_wait(barrier, n - 1 + tp - 1)


def step_kernel(
    n, tp, a_ref, b_ref, x_ref, g_ref, id_ref, live_ref,
    down_out, b_out, grad_a, grad_b, x_out,
    fa, fb, sa, sb, za, zb, ga, gb, pick_a, xt, g, ids, part, gx,
    raw_send, raw_recv, z_send, z_recv, grad_send, grad_recv, far_send, far_recv,
    id_send, id_recv, x_send, x_recv, part_send, part_recv, gx_send, gx_recv, local_sem,
):
    me, mine = lax.axis_index("seq"), lax.axis_index("tp")
    planes = n // GROUP
    plane, spot = me // GROUP, lax.rem(me, GROUP)
    near = me + 1 - 2 * lax.rem(spot, 2)
    far = me + 2 - 4 * (spot // 2)
    far_spot = spot + 2 - 4 * (spot // 2)
    rows = a_ref.shape[0]
    rank = pick_a.shape[0]
    total = fa.shape[0]
    width = xt.shape[2]
    tokens = g.shape[0]
    slots = rows // rank
    column = planes * rank
    f32, low = jnp.float32, jnp.bfloat16

    def remote(src, dst, send, recv, seq_at, tp_at):
        return pltpu.make_async_remote_copy(
            src_ref=src, dst_ref=dst, send_sem=send, recv_sem=recv,
            device_id=(seq_at, tp_at), device_id_type=MESH,
        )

    def columns(index):
        return pl.ds(pl.multiple_of(index * width, width), width)

    own = pl.ds(pl.multiple_of(spot * rows, rows), rows)
    other = pl.ds(pl.multiple_of(far_spot * rows, rows), rows)
    local = [
        pltpu.make_async_copy(a_ref, fa.at[own, :], local_sem.at[0]),
        pltpu.make_async_copy(b_ref, fb.at[own, :], local_sem.at[1]),
        pltpu.make_async_copy(x_ref.at[:, columns(mine)], xt.at[mine], local_sem.at[2]),
        pltpu.make_async_copy(g_ref, g, local_sem.at[3]),
    ]
    for copy in local:
        copy.start()
    greet(n, tp, me, mine)

    def id_copy(d):
        return remote(id_ref, ids.at[me], id_send.at[d], id_recv.at[d], lax.rem(me + d, n), mine)

    lax.fori_loop(1, n, lambda d, c: (id_copy(d).start(), c)[1], 0)

    a_cuts, b_cuts = pieces(a_ref.shape[1], 2), pieces(b_ref.shape[1], 7)
    cuts = [(a_ref, fa, sa, za, *cut) for cut in a_cuts] + [(b_ref, fb, sb, zb, *cut) for cut in b_cuts]
    to_far, to_near, forward = [], [], []
    for j, (src, full, _, _, start, size) in enumerate(cuts):
        cols = pl.ds(start, size)
        to_far.append(remote(src.at[:, cols], full.at[own, cols], raw_send.at[0, j], raw_recv.at[0, j], far, mine))
        to_near.append(remote(src.at[:, cols], full.at[own, cols], raw_send.at[1, j], raw_recv.at[1, j], near, mine))
        forward.append(remote(full.at[other, cols], full.at[other, cols], raw_send.at[2, j], raw_recv.at[2, j], near, mine))
        to_far[j].start()
        to_near[j].start()
    x_copies = []
    for d in range(1, tp):
        peer = lax.rem(mine + d, tp)
        x_copies.append(remote(x_ref.at[:, columns(peer)], xt.at[mine], x_send.at[d], x_recv.at[d], me, peer))
        x_copies[-1].start()
    ids[me] = id_ref[...]
    for copy in local:
        copy.wait()
    lax.fori_loop(1, n, lambda d, c: (id_copy(d).wait(), c)[1], 0)

    base = plane * (total // rank)
    row_at = lax.broadcasted_iota(jnp.int32, (rank, total), 0)
    col_at = lax.broadcasted_iota(jnp.int32, (rank, total), 1)
    picks = []
    for p in range(planes):
        wanted = jnp.broadcast_to(ids[p * GROUP + spot, 0:1, 0:1], (rank, total)) - base
        picks.append((col_at == wanted * rank + row_at).astype(f32))
    pick = jnp.concatenate(picks, axis=0).astype(low)
    place_row = lax.broadcasted_iota(jnp.int32, (rows, n * rank), 0)
    place_col = lax.broadcasted_iota(jnp.int32, (rows, n * rank), 1)
    target = jnp.full((rows, n * rank), -1, jnp.int32)
    for p in range(planes):
        for q in range(GROUP):
            first = (q * planes + p) * rank
            home = jnp.broadcast_to(ids[p * GROUP + q, 1:2, 0:1], (rows, n * rank))
            at = (home - me * slots) * rank + place_col - first
            target = jnp.where((place_col >= first) & (place_col < first + rank), at, target)
    place = (target == place_row).astype(f32).astype(low)

    z_copies = []

    def choose(j):
        _, full, chosen, landed, start, size = cuts[j]
        cols = pl.ds(start, size)
        to_far[j].wait_recv()
        forward[j].start()
        to_near[j].wait_recv()
        forward[j].wait_recv()
        got = jnp.dot(pick, full[:, cols], preferred_element_type=f32).astype(low)
        chosen[:, :, cols] = got.reshape(planes, rank, size)
        for d in range(1, planes):
            to = lax.rem(plane + d, planes)
            copy = remote(
                chosen.at[to, :, cols], landed.at[d, :, cols],
                z_send.at[d, j], z_recv.at[d, j], to * GROUP + spot, mine,
            )
            copy.start()
            z_copies.append(copy)

    def settle(j, out):
        _, _, chosen, landed, start, size = cuts[j]
        cols = pl.ds(start, size)
        value = chosen[plane, :, cols].astype(f32)
        for d in range(1, planes):
            z_copies[j * (planes - 1) + d - 1].wait_recv()
            value += landed[d, :, cols].astype(f32)
        out[:, cols] = value.astype(low)

    def outer(left, right):
        return lax.dot_general(left, right, (((1,), (1,)), ((), ())), preferred_element_type=f32)

    part_copies = []

    def share(which, value):
        part[which, 0] = value
        for d in range(1, tp):
            copy = remote(
                part.at[which, 0], part.at[which, d], part_send.at[which, d], part_recv.at[which, d],
                me, lax.rem(mine + d, tp),
            )
            copy.start()
            part_copies.append(copy)

    def collect(which):
        value = part[which, 0]
        for d in range(1, tp):
            part_copies[which * (tp - 1) + d - 1].wait_recv()
            value = value + part[which, d]
        return value * live_ref[0:1, :]

    grads = [(gb, grad_b, *cut) for cut in b_cuts] + [(ga, grad_a, *cut) for cut in a_cuts]
    slot = pl.ds(pl.multiple_of(spot * column + plane * rank, rank), rank)
    mine_all = pl.ds(pl.multiple_of(spot * column, column), column)
    other_all = pl.ds(pl.multiple_of(far_spot * column, column), column)
    count = len(grads)
    spread_copies = [[] for _ in range(count)]
    far_copies, near_copies, pass_copies = [], [], []

    def spread(j):
        full, _, start, size = grads[j]
        cols = pl.ds(start, size)
        for d in range(1, planes):
            copy = remote(
                full.at[slot, cols], full.at[slot, cols], grad_send.at[d, j], grad_recv.at[d, j],
                lax.rem(plane + d, planes) * GROUP + spot, mine,
            )
            copy.start()
            spread_copies[j].append(copy)

    def cross(j):
        full, _, start, size = grads[j]
        cols = pl.ds(start, size)
        for copy in spread_copies[j]:
            copy.wait_recv()
        far_copies.append(remote(full.at[mine_all, cols], full.at[mine_all, cols], far_send.at[0, j], far_recv.at[0, j], far, mine))
        near_copies.append(remote(full.at[mine_all, cols], full.at[mine_all, cols], far_send.at[1, j], far_recv.at[1, j], near, mine))
        pass_copies.append(remote(full.at[other_all, cols], full.at[other_all, cols], far_send.at[2, j], far_recv.at[2, j], near, mine))
        far_copies[j].start()
        near_copies[j].start()

    def pass_on(j):
        far_copies[j].wait_recv()
        pass_copies[j].start()

    def finish(j):
        full, out, start, size = grads[j]
        cols = pl.ds(start, size)
        near_copies[j].wait_recv()
        pass_copies[j].wait_recv()
        out[:, cols] = jnp.dot(place, full[:, cols], preferred_element_type=f32)

    na, nb = len(a_cuts), len(b_cuts)
    for j in range(na + 2):
        choose(j)
    for j in range(na):
        settle(j, pick_a)
    for copy in x_copies:
        copy.wait()
    x_all = xt[...].reshape(tokens, width)
    share(0, outer(pick_a[...], x_all))
    choose(na + 2)
    down = collect(0).astype(low)
    down_out[...] = down
    for start, size in b_cuts:
        cols = pl.ds(start, size)
        gb[slot, cols] = (adapter_scale * jnp.dot(down, g[:, cols], preferred_element_type=f32)).astype(low)
    sent = 0
    for j in range(na + 3, na + nb):
        spread(sent)
        sent += 1
        choose(j)
    crossed = 0
    early = min(2, sent)
    for j in range(early):
        cross(j)
    crossed = early
    spread(sent)
    sent += 1
    total_back = jnp.zeros((rank, tokens), f32)
    for j in range(nb):
        settle(na + j, b_out)
        cols = pl.ds(*b_cuts[j])
        total_back = total_back + outer(b_out[:, cols], g[:, cols])
    share(1, total_back)
    while sent < nb:
        spread(sent)
        sent += 1
    while crossed < min(nb, 4):
        cross(crossed)
        crossed += 1
    back_full = adapter_scale * collect(1)
    back = back_full.astype(low)
    ga[slot, :] = jnp.dot(back, x_all, preferred_element_type=f32).astype(low)
    for j in range(nb, count):
        spread(j)
    back_t = back_full.T.astype(low)
    gx[...] = jnp.dot(back_t, pick_a[...], preferred_element_type=f32).astype(low).reshape(gx.shape)
    gx_copies = []
    for d in range(1, tp):
        peer = lax.rem(mine + d, tp)
        gx_copies.append(remote(gx.at[peer], x_out.at[:, columns(mine)], gx_send.at[d], gx_recv.at[d], me, peer))
        gx_copies[-1].start()
    x_out[:, columns(mine)] = gx[mine]
    passed, done = 0, 0
    while done < count:
        if crossed < count:
            cross(crossed)
            crossed += 1
        if passed < count and passed < crossed - (1 if crossed < count else 0):
            pass_on(passed)
            passed += 1
        if crossed == count:
            while passed < count and passed - done < 2:
                pass_on(passed)
                passed += 1
            finish(done)
            done += 1
        elif done < passed - 1:
            finish(done)
            done += 1
    for copy in gx_copies:
        copy.wait()
    for copy in to_far + to_near + forward + z_copies + part_copies:
        copy.wait_send()
    for group in spread_copies + [far_copies, near_copies, pass_copies]:
        for copy in group:
            copy.wait_send()


def step(n, tp, a, b, x, g, ids, live):
    slots, rank, width = a.shape
    hidden = b.shape[2]
    rows = x.shape[0]
    tokens = g.shape[0]
    planes = n // GROUP
    cuts = len(pieces(width, 2)) + len(pieces(hidden, 7))
    total = GROUP * slots * rank
    low, f32 = jnp.bfloat16, jnp.float32
    dma = pltpu.SemaphoreType.DMA
    anywhere = pl.BlockSpec(memory_space=pl.ANY)
    inside = pl.BlockSpec(memory_space=VMEM)
    return pl.pallas_call(
        functools.partial(step_kernel, n, tp),
        out_shape=(
            jax.ShapeDtypeStruct((rank, tokens), low),
            jax.ShapeDtypeStruct((rank, hidden), low),
            jax.ShapeDtypeStruct((slots * rank, width), f32),
            jax.ShapeDtypeStruct((slots * rank, hidden), f32),
            jax.ShapeDtypeStruct((rows, tp * width), low),
        ),
        in_specs=[anywhere] * 4 + [inside] * 2,
        out_specs=(inside,) * 5,
        scratch_shapes=[
            VMEM((total, width), low), VMEM((total, hidden), low),
            VMEM((planes, rank, width), low), VMEM((planes, rank, hidden), low),
            VMEM((planes, rank, width), low), VMEM((planes, rank, hidden), low),
            VMEM((n * rank, width), low), VMEM((n * rank, hidden), low),
            VMEM((rank, width), low), VMEM((tp, rows, width), low), VMEM((tokens, hidden), low),
            VMEM((n, 8, 128), jnp.int32), VMEM((2, tp, rank, tokens), f32), VMEM((tp, rows, width), low),
            dma((3, cuts)), dma((3, cuts)), dma((planes, cuts)), dma((planes, cuts)),
            dma((planes, cuts)), dma((planes, cuts)), dma((3, cuts)), dma((3, cuts)),
            dma((n,)), dma((n,)), dma((tp,)), dma((tp,)), dma((2, tp)), dma((2, tp)),
            dma((tp,)), dma((tp,)), dma((4,)),
        ],
        compiler_params=pltpu.CompilerParams(
            collective_id=0, has_side_effects=True, vmem_limit_bytes=56 * 1024 * 1024
        ),
    )(a.reshape(slots * rank, width), b.reshape(slots * rank, hidden), x, g, ids, live)


def per_device(
    normed_input,
    output_gradient,
    adapter_down,
    adapter_up,
    adapter_of_block,
    live_per_block,
    adapter_home_row,
):
    n, tp = lax.axis_size("seq"), lax.axis_size("tp")
    slots, rank, width = adapter_down.shape
    hidden = adapter_up.shape[2]
    tokens = output_gradient.shape[0]
    adapters = adapter_home_row.shape[0]
    f32, low = jnp.float32, jnp.bfloat16
    adapter = adapter_of_block[0]
    home = jnp.sum(jnp.where(jnp.arange(adapters, dtype=jnp.int32) == adapter, adapter_home_row, 0))
    ids = jnp.where(jnp.arange(8, dtype=jnp.int32)[:, None] == 0, adapter, home)
    ids = jnp.broadcast_to(ids, (8, 128))
    live = (jnp.arange(tokens, dtype=jnp.int32) < live_per_block[0]).astype(f32)
    live = jnp.broadcast_to(live[None, :], (8, tokens))
    down, pick_b, grad_a, grad_b, gx = step(
        n, tp, adapter_down, adapter_up, normed_input, output_gradient, ids, live
    )
    out = (adapter_scale * jnp.einsum("rt,rf->tf", down, pick_b, preferred_element_type=f32)).astype(low)
    return (out, gx, grad_a.reshape(slots, rank, width), grad_b.reshape(slots, rank, hidden))


def solution(mesh):
    placed = (
        P(("seq", "tp"), None),
        P("seq", "tp"),
        P("seq", None, "tp"),
        P("seq", None, "tp"),
        P("seq"),
        P("seq"),
        P(),
    )
    return jax.shard_map(
        per_device,
        mesh=mesh,
        in_specs=placed,
        out_specs=(
            P("seq", "tp"),
            P(("seq", "tp"), None),
            P("seq", None, "tp"),
            P("seq", None, "tp"),
        ),
        check_vma=False,
    )
```

time: 335 us -> 91 us (0.27)
  waiting for transfers between devices: 219 us -> 0 us
  Pallas kernels: 0 us -> 79.8 us
  matrix products: 46.4 us -> 2.98 us
  blocking collectives: 37.4 us -> 0 us
  between operations: 15.2 us -> 1.97 us
  starting transfers between devices: 7.36 us -> 0 us
  local copies, waits for them, and re-layouts: 9.02 us -> 4.08 us
    all_gather x4 -> x0, waiting for transfers between devices: 212 us -> none  [the longest x1 107 us: per_device(): lax.all_gather(adapter_up, 'seq', axis=0, tiled=True)]
    pallas_call x0 -> x1, Pallas kernels: none -> 79.8 us  [step(): pl.pallas_call(functools.partial(step_kernel, n, tp), out_shape=(jax.Shap...]
    dot_general x10 -> x1, matrix products: 46.4 us -> 2.98 us  [per_device(): jnp.einsum('rt,rf->tf', down, pick_b, preferred_element_type=f32)]
    unnamed x1 -> x0, blocking collectives: 31.4 us -> none
    all_to_all x2 -> x0, starting transfers between devices: 7.2 us -> none  [the longest x1 3.71 us: per_device(): lax.all_to_all(grad_tensor, 'tp', split_axis=0, concat_axis=1, tiled=True)]
    psum x1 -> x0, blocking collectives: 6.04 us -> none  [per_device(): down_sum, backward_total = lax.psum((down_part, back_part), 'tp')]
    all_to_all x2 -> x0, waiting for transfers between devices: 5.15 us -> none  [the longest x1 5.15 us: per_device(): lax.all_to_all(grad_tensor, 'tp', split_axis=0, concat_axis=1, tiled=True)]
  transfers between devices with their start and end apart: 6 -> 0, of which waited for: 4 -> 0; matrix products, arithmetic and copies ran while one was open for 6% -> 0% of each run, Pallas kernels for 0% -> 0%
where the time goes in v2:
time: 91 us; the launch traced here: 90.8 us
  Pallas kernels  79.8 us (88%)
  local copies, waits for them, and re-layouts  4.08 us (4%)
  matrix products  2.98 us (3%)
  between operations  1.97 us (2%)
  other arithmetic  1.95 us (2%)
    pallas_call x1, Pallas kernels, step(): pl.pallas_call(functools.partial(step_kernel, n, tp), out_shape=(jax.Shap...  79.8 us
    dot_general x1, matrix products, per_device(): jnp.einsum('rt,rf->tf', down, pick_b, preferred_element_type=f32)  2.98 us
    unnamed x9, local copies, waits for them, and re-layouts  2.83 us

profile of v2, /device:TPU:1, one launch (start us, length us, event | category | flops | bytes accessed | tf_op | source)
XLA Modules:
  0.0 90.8 jit_solution(12068702866756958323)
XLA Ops:
  1.9 1.3 %fusion.1 = s32[]{:T(128)} fusion(s32[64]{0:T(128)} %param.13, s32[]{:T(128)} %bitcast.9), kind=kLoop, calls=%fused_computation.5 | loop fusion | flops 191 | bytes 264 | tf_op jit(solution)/shard_map/reduce_sum | solution.py:350
  3.2 0.6 compare_select_fusion.1
  3.9 0.7 broadcast_in_dim.27.id_ref
  4.5 0.6 broadcast_in_dim.28.live_ref
  5.1 79.8 %shard_map.102 = (bf16[16,128]{1,0:T(8,128)(2,1)}, bf16[16,7168]{1,0:T(8,128)(2,1)}, f32[64,2048]{1,0:T(8,128)}, f32[64,7168]{1,0:T(8,128)}, bf16[64,4096]{1,0:T(8,128)(2,1)}) custom-call(bf16[64,2048]{1,0:T(8,128)(2,1)} %bitcast.14, bf16[64,7168]{1,0:T(8,128)(2,1)} %bitcast.12, bf16[64,4096]{1,0:T(8,128)(2,1)} %x_ref.1, bf16[128,7168]{1,0:T(8,128)(2,1)} %g_ref.1, ...), custom_call_target="tpu_custom_call" | custom-call | tf_op jit(solution)/shard_map/pallas_call | solution.py:305
  85.0 0.0 copy-start.2
  85.0 0.0 copy-start.1
  85.0 0.0 copy-start
  85.0 3.0 %fusion = bf16[128,7168]{1,0:T(8,128)(2,1)} fusion(bf16[16,128]{1,0:T(8,128)(2,1)} %get-tuple-element.9, bf16[16,7168]{1,0:T(8,128)(2,1)} %get-tuple-element.10), kind=kOutput, calls=%fused_computation.1 | convolution fusion | flops 31195136 | bytes 2068480 | tf_op jit(solution)/shard_map/rt,rf->tf/dot_general | solution.py:358
  88.0 0.0 copy-done.2
  88.0 0.8 copy.16
  88.8 0.0 copy-done.1
  88.8 0.8 copy.17
  89.6 0.0 copy-done
  89.6 1.2 %copy.18 = f32[4,16,7168]{2,1,0:T(8,128)} copy(f32[4,16,7168]{2,1,0:T(8,128)S(1)} %bitcast.11) | data formatting | bytes 3670016
  (1 shorter events, 0.0 us)
Async XLA Ops:
  85.0 3.0 %copy-start.2 = (bf16[64,4096]{1,0:T(8,128)(2,1)S(1)}, bf16[64,4096]{1,0:T(8,128)(2,1)}, u32[]{:S(2)}) copy-start(bf16[64,4096]{1,0:T(8,128)(2,1)} %get-tuple-element.19) | copy-start | bytes 1572868
  85.0 3.8 %copy-start.1 = (f32[64,2048]{1,0:T(8,128)S(1)}, f32[64,2048]{1,0:T(8,128)}, u32[]{:S(2)}) copy-start(f32[64,2048]{1,0:T(8,128)} %get-tuple-element.12) | copy-start | bytes 1572868
  85.0 4.6 %copy-start = (f32[64,7168]{1,0:T(8,128)S(1)}, f32[64,7168]{1,0:T(8,128)}, u32[]{:S(2)}) copy-start(f32[64,7168]{1,0:T(8,128)} %get-tuple-element.13) | copy-start | bytes 5505028

commit v3 on v2

--- a/solution.py
+++ b/solution.py
@@ -176,25 +176,56 @@
     mine_all = pl.ds(pl.multiple_of(spot * column, column), column)
     other_all = pl.ds(pl.multiple_of(far_spot * column, column), column)
     count = len(grads)
-    spread_copies = [[] for _ in range(count)]
     far_copies, near_copies, pass_copies = [], [], []
 
+    def hop(source, side, j):
+        full, _, start, size = grads[j]
+        at = pl.ds(pl.multiple_of(spot * column + source * rank, rank), rank)
+        view = full.at[at, pl.ds(start, size)]
+        to = lax.rem(plane + (1 if side == 0 else planes - 1), planes)
+        return remote(view, view, grad_send.at[2 * source + side, j], grad_recv.at[source, j], to * GROUP + spot, mine)
+
     def spread(j):
-        full, _, start, size = grads[j]
-        cols = pl.ds(start, size)
+        @pl.when(plane < planes - 1)
+        def _():
+            hop(plane, 0, j).start()
+
+        @pl.when(plane > 0)
+        def _():
+            hop(plane, 1, j).start()
+
+    def relay(j):
         for d in range(1, planes):
-            copy = remote(
-                full.at[slot, cols], full.at[slot, cols], grad_send.at[d, j], grad_recv.at[d, j],
-                lax.rem(plane + d, planes) * GROUP + spot, mine,
-            )
-            copy.start()
-            spread_copies[j].append(copy)
+            @pl.when(plane >= d)
+            def _():
+                hop(plane - d, 0, j).wait_recv()
+
+                @pl.when(plane < planes - 1)
+                def _():
+                    hop(plane - d, 0, j).start()
+
+            @pl.when(plane + d < planes)
+            def _():
+                hop(plane + d, 1, j).wait_recv()
+
+                @pl.when(plane > 0)
+                def _():
+                    hop(plane + d, 1, j).start()
+
+    def relay_end(j):
+        for d in range(planes):
+            @pl.when((plane >= d) & (plane < planes - 1))
+            def _():
+                hop(plane - d, 0, j).wait_send()
+
+            @pl.when((plane + d < planes) & (plane > 0))
+            def _():
+                hop(plane + d, 1, j).wait_send()
 
     def cross(j):
         full, _, start, size = grads[j]
         cols = pl.ds(start, size)
-        for copy in spread_copies[j]:
-            copy.wait_recv()
+        relay(j)
         far_copies.append(remote(full.at[mine_all, cols], full.at[mine_all, cols], far_send.at[0, j], far_recv.at[0, j], far, mine))
         near_copies.append(remote(full.at[mine_all, cols], full.at[mine_all, cols], far_send.at[1, j], far_recv.at[1, j], near, mine))
         pass_copies.append(remote(full.at[other_all, cols], full.at[other_all, cols], far_send.at[2, j], far_recv.at[2, j], near, mine))
@@ -285,7 +316,9 @@
         copy.wait()
     for copy in to_far + to_near + forward + z_copies + part_copies:
         copy.wait_send()
-    for group in spread_copies + [far_copies, near_copies, pass_copies]:
+    for j in range(count):
+        relay_end(j)
+    for group in [far_copies, near_copies, pass_copies]:
         for copy in group:
             copy.wait_send()
 
@@ -321,7 +354,7 @@
             VMEM((rank, width), low), VMEM((tp, rows, width), low), VMEM((tokens, hidden), low),
             VMEM((n, 8, 128), jnp.int32), VMEM((2, tp, rank, tokens), f32), VMEM((tp, rows, width), low),
             dma((3, cuts)), dma((3, cuts)), dma((planes, cuts)), dma((planes, cuts)),
-            dma((planes, cuts)), dma((planes, cuts)), dma((3, cuts)), dma((3, cuts)),
+            dma((2 * planes, cuts)), dma((planes, cuts)), dma((3, cuts)), dma((3, cuts)),
             dma((n,)), dma((n,)), dma((tp,)), dma((tp,)), dma((2, tp)), dma((2, tp)),
             dma((tp,)), dma((tp,)), dma((4,)),
         ],

time: 91 us -> 94.9 us (1.043)
  Pallas kernels: 79.8 us -> 83.6 us
    pallas_call x1, Pallas kernels: 79.8 us -> 83.6 us  [step(): pl.pallas_call(functools.partial(step_kernel, n, tp), out_shape=(jax.Shap...]
where the time goes in v3:
time: 94.9 us; the launch traced here: 94.6 us
  Pallas kernels  83.6 us (88%)
  local copies, waits for them, and re-layouts  4.08 us (4%)
  matrix products  2.98 us (3%)
  between operations  1.97 us (2%)
  other arithmetic  1.95 us (2%)
    pallas_call x1, Pallas kernels, step(): pl.pallas_call(functools.partial(step_kernel, n, tp), out_shape=(jax.Shap...  83.6 us
    dot_general x1, matrix products, per_device(): jnp.einsum('rt,rf->tf', down, pick_b, preferred_element_type=f32)  2.98 us
    unnamed x9, local copies, waits for them, and re-layouts  2.83 us

profile of v3, /device:TPU:1, one launch (start us, length us, event | category | flops | bytes accessed | tf_op | source)
XLA Modules:
  0.0 94.6 jit_solution(16513542172235715015)
XLA Ops:
  1.9 1.3 %fusion.1 = s32[]{:T(128)} fusion(s32[64]{0:T(128)} %param.13, s32[]{:T(128)} %bitcast.9), kind=kLoop, calls=%fused_computation.5 | loop fusion | flops 191 | bytes 264 | tf_op jit(solution)/shard_map/reduce_sum | solution.py:383
  3.2 0.6 compare_select_fusion.1
  3.9 0.7 broadcast_in_dim.27.id_ref
  4.5 0.6 broadcast_in_dim.28.live_ref
  5.1 83.6 %shard_map.102 = (bf16[16,128]{1,0:T(8,128)(2,1)}, bf16[16,7168]{1,0:T(8,128)(2,1)}, f32[64,2048]{1,0:T(8,128)}, f32[64,7168]{1,0:T(8,128)}, bf16[64,4096]{1,0:T(8,128)(2,1)}) custom-call(bf16[64,2048]{1,0:T(8,128)(2,1)} %bitcast.14, bf16[64,7168]{1,0:T(8,128)(2,1)} %bitcast.12, bf16[64,4096]{1,0:T(8,128)(2,1)} %x_ref.1, bf16[128,7168]{1,0:T(8,128)(2,1)} %g_ref.1, ...), custom_call_target="tpu_custom_call" | custom-call | tf_op jit(solution)/shard_map/pallas_call | solution.py:338
  88.8 0.0 copy-start.2
  88.8 0.0 copy-start.1
  88.8 0.0 copy-start
  88.8 3.0 %fusion = bf16[128,7168]{1,0:T(8,128)(2,1)} fusion(bf16[16,128]{1,0:T(8,128)(2,1)} %get-tuple-element.9, bf16[16,7168]{1,0:T(8,128)(2,1)} %get-tuple-element.10), kind=kOutput, calls=%fused_computation.1 | convolution fusion | flops 31195136 | bytes 2068480 | tf_op jit(solution)/shard_map/rt,rf->tf/dot_general | solution.py:391
  91.8 0.0 copy-done.2
  91.8 0.8 copy.16
  92.6 0.0 copy-done.1
  92.6 0.8 copy.17
  93.4 0.0 copy-done
  93.4 1.2 %copy.18 = f32[4,16,7168]{2,1,0:T(8,128)} copy(f32[4,16,7168]{2,1,0:T(8,128)S(1)} %bitcast.11) | data formatting | bytes 3670016
  (1 shorter events, 0.0 us)
Async XLA Ops:
  88.8 3.0 %copy-start.2 = (bf16[64,4096]{1,0:T(8,128)(2,1)S(1)}, bf16[64,4096]{1,0:T(8,128)(2,1)}, u32[]{:S(2)}) copy-start(bf16[64,4096]{1,0:T(8,128)(2,1)} %get-tuple-element.19) | copy-start | bytes 1572868
  88.8 3.8 %copy-start.1 = (f32[64,2048]{1,0:T(8,128)S(1)}, f32[64,2048]{1,0:T(8,128)}, u32[]{:S(2)}) copy-start(f32[64,2048]{1,0:T(8,128)} %get-tuple-element.12) | copy-start | bytes 1572868
  88.8 4.6 %copy-start = (f32[64,7168]{1,0:T(8,128)S(1)}, f32[64,7168]{1,0:T(8,128)}, u32[]{:S(2)}) copy-start(f32[64,7168]{1,0:T(8,128)} %get-tuple-element.13) | copy-start | bytes 5505028
